TPU v7x, 256 devices: a whole 4x4x8 slice. The times are simulated.
256 devices in a mesh: dp: 8 (over z_lo, core), seq: 16 (over x, y), mp: 2 (over z_hi).
Axes of the slice: x: 4, y: 4, z: 8 (z_hi: 2, z_lo: 4; z = z_hi * 4 + z_lo), core: 2. Of those that a mesh axis runs over, the one named last changes fastest.
Arguments:
- features: bfloat16 [8, 8192, 1408], P('dp', ('seq', 'mp')), may hold values from -6 to 6
- conv_weight: bfloat16 [5, 1408, 1536], P(None, ('seq', 'mp')), may hold values from -0.0625 to 0.0625
- norm_gain: float32 [1536], replicated, may hold values from 0.25 to 1.75
- query_weight: bfloat16 [1536, 1024], replicated, may hold values from -0.15625 to 0.15625
- keyval_weight: bfloat16 [1536, 320], replicated, may hold values from -0.15625 to 0.15625
- head_scale: float32 [8], replicated, may hold values from 0.5 to 24
- output_weight: bfloat16 [1536, 1536], replicated, may hold values from -0.15625 to 0.15625
- pair_weight: bfloat16 [1536, 256], replicated, may hold values from -0.625 to 0.625
- pair_input: bfloat16 [8, 256, 256, 128], P('dp', ('seq', 'mp')), may hold values from -6 to 6
- flip_weight: bfloat16 [128, 128], replicated, may hold values from -0.5 to 0.5
- pair_cotangent: bfloat16 [8, 256, 256, 128], P('dp', ('seq', 'mp')), may hold values from -0.0234375 to 0.0234375
Outputs:
- block_out: bfloat16 [8, 4096, 1536], P('dp', ('seq', 'mp'))
- pair_out: bfloat16 [8, 256, 256, 128], P('dp', ('seq', 'mp'))
- grad_flip: float32 [128, 128], replicated
All inputs are finite; a program needn't handle non-finite values.
Results may differ from a plain program's by a relative error of at most 0.011.
Values may be sent and summed in bfloat16 or wider, within the bound.
A program may use at most 192 MiB of HBM per device.

v0:
```python
import math
import jax
import jax.numpy as jnp
from jax import lax
from jax.sharding import PartitionSpec as P

PAIR_POOL = 16
norm_eps = 1e-06
logit_cap = 50.0


def padded_2(shard, sides, width):
    for axis, dim in sides:
        devices, length = (lax.axis_size(axis), shard.shape[dim])
        up = [(i, (i + 1) % devices) for i in range(devices - 1)]
        down = [(j, i) for i, j in up]
        last = lax.slice_in_dim(shard, length - width, length, axis=dim)
        initial = lax.slice_in_dim(shard, 0, width, axis=dim)
        before = lax.ppermute(last, axis, up)
        after = lax.ppermute(initial, axis, down)
        shard = jnp.concatenate([before, shard, after], axis=dim)
    return shard


def root_norm(values_in):
    return values_in * lax.rsqrt(jnp.mean(values_in * values_in, axis=-1, keepdims=True) + norm_eps)


def prepare(raw):
    return jax.nn.gelu(root_norm(raw.astype(jnp.float32)), approximate=False).astype(jnp.bfloat16)


def tap_sum(source, out_rows, tap_count, running, filter_rows):
    for lag_index in range(tap_count):
        running = running + jnp.dot(
            source[lag_index : lag_index + out_rows],
            filter_rows[lag_index],
            preferred_element_type=jnp.float32,
        )
    return running


def per_device(
    features,
    conv_weight,
    norm_gain,
    query_weight,
    keyval_weight,
    head_scale,
    output_weight,
    pair_weight,
    pair_input,
    flip_weight,
    pair_cotangent,
):
    fine_rows = features.shape[1]
    coarse_rows = fine_rows // 2
    in_channels = features.shape[2]
    model_dim = output_weight.shape[1]
    head_count = head_scale.shape[0]
    key_dim = query_weight.shape[1] // head_count
    pair_dim = flip_weight.shape[0]
    tap_count = conv_weight.shape[0]
    margin = tap_count // 2
    padded = padded_2(features, ((("seq", "mp"), 1),), margin)
    prepared = prepare(padded[0])
    starting = jnp.zeros((fine_rows, model_dim), jnp.float32)
    conv_sum = tap_sum(
        prepared,
        fine_rows,
        tap_count,
        starting,
        lax.all_gather(conv_weight, ("seq", "mp"), axis=1, tiled=True),
    )
    skipped = jnp.pad(features[0].astype(jnp.float32), ((0, 0), (0, model_dim - in_channels)))
    encoded = jnp.max((conv_sum + skipped).reshape(coarse_rows, 2, model_dim), axis=1).astype(
        jnp.bfloat16
    )
    widened = encoded.astype(jnp.float32)
    normed = (root_norm(widened) * norm_gain).astype(jnp.bfloat16)
    scale_row = jnp.repeat(head_scale, key_dim) / math.sqrt(key_dim)
    queries = (
        jnp.dot(normed, query_weight, preferred_element_type=jnp.float32) * scale_row
    ).astype(jnp.bfloat16)
    keyvals = jnp.dot(normed, keyval_weight, preferred_element_type=jnp.float32).astype(
        jnp.bfloat16
    )
    pooled = jnp.mean(
        widened.reshape(coarse_rows // PAIR_POOL, PAIR_POOL, model_dim), axis=1
    ).astype(jnp.bfloat16)
    pair_feats = jnp.dot(pooled, pair_weight, preferred_element_type=jnp.float32).astype(
        jnp.bfloat16
    )
    pair_q = pair_feats[:, :pair_dim]
    pair_k = pair_feats[:, pair_dim:]
    keys_all, pairk_all = (
        lax.all_gather(keyvals[None], ("seq", "mp"), axis=1, tiled=True),
        lax.all_gather(pair_k[None], ("seq", "mp"), axis=1, tiled=True),
    )
    summed = (
        pair_input[0].astype(jnp.float32)
        + pair_q[:, None, :].astype(jnp.float32) * pairk_all[0][None, :, :].astype(jnp.float32)
    ).astype(jnp.bfloat16)
    flipped = lax.all_to_all(summed[None], ("seq", "mp"), split_axis=2, concat_axis=1, tiled=True)[
        0
    ]
    turned = jnp.einsum("bac,cd->abd", flipped, flip_weight, preferred_element_type=jnp.float32)
    pair_out = (summed.astype(jnp.float32) + turned).astype(jnp.bfloat16)
    grad_term = jnp.einsum(
        "bac,abd->cd", flipped, pair_cotangent[0], preferred_element_type=jnp.float32
    )
    grad_flip = lax.psum(grad_term, ("dp", "seq", "mp"))
    key_rows = keys_all[0][:, :key_dim]
    value_rows = keys_all[0][:, key_dim:]
    query_rows = queries.reshape(coarse_rows * head_count, key_dim)
    scores = jnp.dot(query_rows, key_rows.T, preferred_element_type=jnp.float32)
    weights = jnp.exp(logit_cap * jnp.tanh(scores / logit_cap))
    totals = jnp.sum(weights, axis=-1, keepdims=True)
    mixed = (
        jnp.dot(weights.astype(jnp.bfloat16), value_rows, preferred_element_type=jnp.float32)
        / totals
    )
    heads_out = mixed.astype(jnp.bfloat16).reshape(coarse_rows, head_count * value_rows.shape[1])
    block_out = (
        widened + jnp.dot(heads_out, output_weight, preferred_element_type=jnp.float32)
    ).astype(jnp.bfloat16)
    return (block_out[None], pair_out[None], grad_flip)


def solution(mesh):
    placed = (
        P("dp", ("seq", "mp"), None),
        P(None, ("seq", "mp"), None),
        P(),
        P(),
        P(),
        P(),
        P(),
        P(),
        P("dp", ("seq", "mp"), None, None),
        P(),
        P("dp", ("seq", "mp"), None, None),
    )
    return jax.shard_map(
        per_device,
        mesh=mesh,
        in_specs=placed,
        out_specs=(P("dp", ("seq", "mp"), None), P("dp", ("seq", "mp"), None, None), P()),
        check_vma=False,
    )
```

profile of v0, /device:TPU:1, one launch (start us, length us, event | category | flops | bytes accessed | tf_op | source)
XLA Modules:
  0.0 959.2 jit_solution(9439417309653292819)
XLA Ops:
  7.2 0.0 copy-start
  7.2 0.0 all-gather.5.cloned.1.call-start
  7.2 2.7 copy.24
  9.9 0.0 all-gather.5.cloned.1.call-update
  9.9 0.0 all-gather.7.cloned.1.call-start
  10.0 0.8 fusion.84
  10.7 1.3 collective-permute-start.1
  12.0 10.3 %collective-permute-start = (bf16[1,2,1408]{2,1,0:T(2,128)(2,1)S(1)}, bf16[1,2,1408]{2,1,0:T(2,128)(2,1)S(1)}, u32[]{:S(2)}, u32[]{:S(2)}) collective-permute-start(bf16[1,2,1408]{2,1,0:T(2,128)(2,1)S(1)} %get-tuple-element.8), channel_id=1, source_target_pairs={{0,1},{1,2},{2,3},{3,4},{4,5},{5,6},{6,7},{7,8},{8,9},{9,10},{10,1... | collective-permute-start | bytes 16904 | tf_op jit(solution)/shard_map/ppermute | solution.py:19
  22.3 0.0 collective-permute-done.1
  22.3 0.7 collective-permute-done
  23.1 1.4 fusion.48
  24.5 6.0 fusion.20
  30.5 426.3 %all-gather.5.cloned.1.call-done = bf16[5,1408,1536]{2,0,1:T(8,128)(2,1)} async-done(((bf16[5,44,1536]{2,0,1:T(8,128)(2,1)}), bf16[5,1408,1536]{2,0,1:T(8,128)(2,1)}) %all-gather.5.cloned.1.call-update) | async-done | bytes 21626896 | tf_op jit(solution)/shard_map/all_gather | solution.py:73
  456.8 0.0 copy-start.4
  456.8 92.6 %fusion.83 = (bf16[1,1408,1536]{2,0,1:T(2,128)(2,1)S(1)}, bf16[1,1408,1536]{2,0,1:T(2,128)(2,1)S(1)}, bf16[1,1408,1536]{2,0,1:T(2,128)(2,1)}, bf16[1,1408,1536]{2,0,1:T(2,128)(2,1)}, bf16[1,1408,1536]{2,0,1:T(2,128)(2,1)}) fusion(bf16[5,1408,1536]{2,0,1:T(8,128)(2,1)} %all-gather.5.cloned.1.call-done), kind=kLoop, calls=%fused_computation.101 | loop fusion | bytes 43253760 | tf_op jit(solution)/shard_map/slice | solution.py:37
  549.4 0.0 copy-done.4
  549.4 0.0 slice-start.1
  549.4 5.0 fusion.7
  554.4 0.0 slice-start.2
  554.5 4.9 fusion.9
  559.4 0.0 slice-done
  559.4 0.0 slice-done.1
  559.4 0.0 slice-done.2
  559.4 1.4 fusion.10
  560.8 0.0 copy-start.1
  560.8 1.4 fusion.11
  562.2 0.0 copy-done.1
  562.3 2.3 fusion.13
  564.6 2.9 reshape.58
  567.5 3.0 reduce_max.9
  570.5 0.2 multiply_reduce_fusion
  570.7 0.0 copy-done.5
  570.7 2.3 convolution_convert_fusion
  573.0 0.0 all-gather.7.cloned.1.call-update
  573.0 0.0 copy-start.2
  573.0 0.1 bitcast_reduce_fusion
  573.2 1.4 convolution_convert_fusion.1
  574.6 105.2 %all-gather.1 = bf16[256,128]{1,0:T(8,128)(2,1)S(1)} all-gather(bf16[8,128]{1,0:T(8,128)(2,1)S(1)} %get-tuple-element.11), channel_id=3, replica_groups=mesh['dp'=8,'seq'=16,'mp'=2] {'seq','mp'}, dimensions={0}, use_global_device_ids=true | all-gather | bytes 67584 | tf_op jit(solution)/shard_map/all_gather | solution.py:98
  679.8 0.0 copy-start.3
  679.8 0.0 copy-done.2
  679.8 0.1 fusion.55
  680.0 0.5 copy-done.3
  680.5 1.1 copy.31
  681.6 4.6 all-to-all-start
  686.2 0.0 all-reduce.3.cloned.1.call-start
  686.3 0.7 broadcast_multiply_fusion
  686.9 0.1 broadcast_bitcast_fusion
  687.0 0.0 copy-done
  687.0 1.3 fusion.52
  688.3 1.8 reshape.59
  690.1 9.7 %all-to-all-done = bf16[1,8,256,128]{3,1,0,2:T(8,128)(2,1)} async-done(((bf16[1,8,256,128]{3,1,0,2:T(8,128)(2,1)}), bf16[1,8,256,128]{3,1,0,2:T(8,128)(2,1)}, u32[]{:S(2)}, u32[]{:S(2)}) %all-to-all-start) | async-done | bytes 524320 | tf_op jit(solution)/shard_map/all_to_all | solution.py:104
  699.8 2.2 convolution_bitcast_fusion.1
  702.0 2.3 fusion.51
  704.4 0.0 all-reduce.3.cloned.1.call-update
  704.4 0.0 all-gather.7.cloned.1.call-done
  704.4 0.0 copy-start.6
  704.4 6.7 fusion
  711.1 0.0 copy-done.6
  711.1 5.9 fusion.63
  717.0 2.0 copy.30
  719.0 2.3 reshape.60
  721.3 4.0 fusion.15
  725.3 225.9 %all-reduce.3.cloned.1.call-done = f32[128,128]{1,0:T(8,128)} async-done(((f32[128,128]{1,0:T(8,128)}), f32[128,128]{1,0:T(8,128)}) %all-reduce.3.cloned.1.call-update) | async-done | bytes 65552 | tf_op jit(solution)/shard_map/psum | solution.py:112
  951.2 1.5 copy.69
  (7 shorter events, 0.0 us)
Async XLA Ops:
  7.2 679.8 %copy-start = (bf16[1536,1024]{1,0:T(8,128)(2,1)S(1)}, bf16[1536,1024]{1,0:T(8,128)(2,1)}, u32[]{:S(2)}) copy-start(bf16[1536,1024]{1,0:T(8,128)(2,1)} %param.14) | copy-start | bytes 9437188
  7.2 449.6 %all-gather.5.cloned.1.call-start = ((), (), s32[]{:S(2)}) async-start(), calls=%async_computation.1 | async-start | bytes 35684352 | tf_op jit(solution)/shard_map/all_gather | solution.py:73
  9.9 694.5 %all-gather.7.cloned.1.call-start = ((), (), s32[]{:S(2)}) async-start(), calls=%async_computation.3 | async-start | bytes 2703360 | tf_op jit(solution)/shard_map/all_gather | solution.py:97
  10.7 11.6 %collective-permute-start.1 = (bf16[1,2,1408]{2,1,0:T(2,128)(2,1)S(1)}, bf16[1,2,1408]{2,1,0:T(2,128)(2,1)S(1)}, u32[]{:S(2)}, u32[]{:S(2)}) collective-permute-start(bf16[1,2,1408]{2,1,0:T(2,128)(2,1)S(1)} %get-tuple-element.9), channel_id=1, source_target_pairs={{1,0},{2,1},{3,2},{4,3},{5,4},{6,5},{7,6},{8,7},{9,8},{10,9},{11,1... | collective-permute-start | bytes 16904 | tf_op jit(solution)/shard_map/ppermute | solution.py:20
  12.0 11.0 %collective-permute-start = (bf16[1,2,1408]{2,1,0:T(2,128)(2,1)S(1)}, bf16[1,2,1408]{2,1,0:T(2,128)(2,1)S(1)}, u32[]{:S(2)}, u32[]{:S(2)}) collective-permute-start(bf16[1,2,1408]{2,1,0:T(2,128)(2,1)S(1)} %get-tuple-element.8), channel_id=1, source_target_pairs={{0,1},{1,2},{2,3},{3,4},{4,5},{5,6},{6,7},{7,8},{8,9},{9,10},{10,1... | collective-permute-start | bytes 16904 | tf_op jit(solution)/shard_map/ppermute | solution.py:19
  456.8 92.6 %copy-start.4 = (bf16[260,1408]{1,0:T(8,128)(2,1)S(1)}, bf16[260,1408]{1,0:T(8,128)(2,1)}, u32[]{:S(2)}) copy-start(bf16[260,1408]{1,0:T(8,128)(2,1)} %fusion.20) | copy-start | bytes 2196484
  549.4 9.9 %slice-start = ((s8[8650752]{0:T(1024)(128)(4,1)}), s8[4194304]{0:T(1024)(128)(4,1)S(1)}, s32[]{:S(2)}) async-start(s8[8650752]{0:T(1024)(128)(4,1)} %bitcast.79), calls=%async_computation.4 | async-start | bytes 8388608
  549.4 9.9 %slice-start.1 = ((s8[8650752]{0:T(1024)(128)(4,1)}), s8[4194304]{0:T(1024)(128)(4,1)S(1)}, s32[]{:S(2)}) async-start(s8[8650752]{0:T(1024)(128)(4,1)} %bitcast.79), calls=%async_computation.5 | async-start | bytes 8388608
  554.4 4.9 slice-start.2
  560.8 1.4 copy-start.1
  564.6 6.1 copy-start.5
  573.0 106.8 %copy-start.2 = (bf16[1,8,256,128]{3,2,1,0:T(8,128)(2,1)S(1)}, bf16[1,8,256,128]{3,2,1,0:T(8,128)(2,1)}, u32[]{:S(2)}) copy-start(bf16[1,8,256,128]{3,2,1,0:T(8,128)(2,1)} %param.19) | copy-start | bytes 1572868
  679.8 0.6 copy-start.3
  681.6 18.2 %all-to-all-start = ((bf16[1,8,256,128]{3,1,0,2:T(8,128)(2,1)}), bf16[1,8,256,128]{3,1,0,2:T(8,128)(2,1)}, u32[]{:S(2)}, u32[]{:S(2)}) async-start(bf16[1,8,256,128]{3,1,0,2:T(8,128)(2,1)} %copy.31), calls=%async_computation | async-start | bytes 1048576 | tf_op jit(solution)/shard_map/all_to_all | solution.py:104
  686.2 264.9 %all-reduce.3.cloned.1.call-start = ((), (), s32[]{:S(2)}) async-start(), calls=%async_computation.2 | async-start | bytes 131072 | tf_op jit(solution)/shard_map/psum | solution.py:112
  704.4 6.7 copy-start.6
Sparse Core Ops, SparseCore 0:
  11.4 445.3 all-gather.4
  573.2 103.0 all-gather.6
  704.5 246.6 all-reduce.2
where the time goes:
time: 960 us; the launch traced here: 959 us
  waiting for transfers between devices  663 us (69%)
  local copies, waits for them, and re-layouts  108 us (11%)
  blocking collectives  105 us (11%)
  matrix products  41.2 us (4%)
  starting transfers between devices  16.3 us (2%)
  between operations  14 us (1%)
  other arithmetic  11.6 us (1%)
    all_gather x1, waiting for transfers between devices, per_device(): lax.all_gather(conv_weight, ('seq', 'mp'), axis=1, tiled=True)  426 us
    psum x1, waiting for transfers between devices, per_device(): grad_flip = lax.psum(grad_term, ('dp', 'seq', 'mp'))  226 us
    all_gather x1, blocking collectives, per_device(): lax.all_gather(pair_k[None], ('seq', 'mp'), axis=1, tiled=True)  105 us
    slice x1, local copies, waits for them, and re-layouts, tap_sum(): filter_rows[lag_index]  92.6 us
  transfers between devices with their start and end apart: 6, of which 4 were waited for; matrix products, arithmetic and copies ran while one was open for 4% of the time, Pallas kernels for 0%

commit v1 on v0

--- a/solution.py
+++ b/solution.py
@@ -7,6 +7,11 @@
 PAIR_POOL = 16
 norm_eps = 1e-06
 logit_cap = 50.0
+
+
+def gather_over(x, axis, along):
+    sent = jnp.stack([x] * lax.axis_size(axis))
+    return jnp.concatenate(lax.all_to_all(sent, axis, 0, 0), axis=along)
 
 
 def padded_2(shard, sides, width):
@@ -95,7 +100,7 @@
     pair_k = pair_feats[:, pair_dim:]
     keys_all, pairk_all = (
         lax.all_gather(keyvals[None], ("seq", "mp"), axis=1, tiled=True),
-        lax.all_gather(pair_k[None], ("seq", "mp"), axis=1, tiled=True),
+        gather_over(pair_k[None], ("seq", "mp"), 1),
     )
     summed = (
         pair_input[0].astype(jnp.float32)

time: 960 us -> 930 us (0.969)
  blocking collectives: 105 us -> 16.5 us
  waiting for transfers between devices: 663 us -> 719 us
    all_gather x1 -> x0, blocking collectives: 105 us -> none  [per_device(): lax.all_gather(pair_k[None], ('seq', 'mp'), axis=1, tiled=True)]
    all_gather x1, waiting for transfers between devices: 0.02 us -> 61.4 us  [per_device(): lax.all_gather(keyvals[None], ('seq', 'mp'), axis=1, tiled=True)]
    all_to_all x0 -> x1, blocking collectives: none -> 16.5 us  [gather_over(): return jnp.concatenate(lax.all_to_all(sent, axis, 0, 0), axis=along)]
  transfers between devices with their start and end apart: 6 -> 6, of which waited for: 4 -> 5; matrix products, arithmetic and copies ran while one was open for 4% -> 4% of each run, Pallas kernels for 0% -> 0%
where the time goes in v1:
time: 930 us; the launch traced here: 929 us
  waiting for transfers between devices  719 us (77%)
  local copies, waits for them, and re-layouts  108 us (12%)
  matrix products  41.2 us (4%)
  starting transfers between devices  18.1 us (2%)
  blocking collectives  16.5 us (2%)
  between operations  14 us (2%)
  other arithmetic  11.6 us (1%)
    all_gather x1, waiting for transfers between devices, per_device(): lax.all_gather(conv_weight, ('seq', 'mp'), axis=1, tiled=True)  426 us
    psum x1, waiting for transfers between devices, per_device(): grad_flip = lax.psum(grad_term, ('dp', 'seq', 'mp'))  220 us
    slice x1, local copies, waits for them, and re-layouts, tap_sum(): filter_rows[lag_index]  92.6 us
    all_gather x1, waiting for transfers between devices, per_device(): lax.all_gather(keyvals[None], ('seq', 'mp'), axis=1, tiled=True)  61.4 us
  transfers between devices with their start and end apart: 6, of which 5 were waited for; matrix products, arithmetic and copies ran while one was open for 4% of the time, Pallas kernels for 0%

profile of v1, /device:TPU:1, one launch (start us, length us, event | category | flops | bytes accessed | tf_op | source)
XLA Modules:
  0.0 929.0 jit_solution(17491234446463642762)
XLA Ops:
  7.2 0.0 copy-start
  7.2 0.0 all-gather.4.cloned.1.call-start
  7.2 2.7 copy.24
  9.9 0.0 all-gather.4.cloned.1.call-update
  9.9 0.0 all-gather.6.cloned.1.call-start
  10.0 0.8 fusion.84
  10.7 1.3 collective-permute-start.1
  12.0 10.3 %collective-permute-start = (bf16[1,2,1408]{2,1,0:T(2,128)(2,1)S(1)}, bf16[1,2,1408]{2,1,0:T(2,128)(2,1)S(1)}, u32[]{:S(2)}, u32[]{:S(2)}) collective-permute-start(bf16[1,2,1408]{2,1,0:T(2,128)(2,1)S(1)} %get-tuple-element.8), channel_id=1, source_target_pairs={{0,1},{1,2},{2,3},{3,4},{4,5},{5,6},{6,7},{7,8},{8,9},{9,10},{10,1... | collective-permute-start | bytes 16904 | tf_op jit(solution)/shard_map/ppermute | solution.py:24
  22.3 0.0 collective-permute-done.1
  22.3 0.7 collective-permute-done
  23.1 1.4 fusion.48
  24.5 6.0 fusion.20
  30.5 426.3 %all-gather.4.cloned.1.call-done = bf16[5,1408,1536]{2,0,1:T(8,128)(2,1)} async-done(((bf16[5,44,1536]{2,0,1:T(8,128)(2,1)}), bf16[5,1408,1536]{2,0,1:T(8,128)(2,1)}) %all-gather.4.cloned.1.call-update) | async-done | bytes 21626896 | tf_op jit(solution)/shard_map/all_gather | solution.py:78
  456.8 0.0 copy-start.4
  456.8 92.6 %fusion.83 = (bf16[1,1408,1536]{2,0,1:T(2,128)(2,1)S(1)}, bf16[1,1408,1536]{2,0,1:T(2,128)(2,1)S(1)}, bf16[1,1408,1536]{2,0,1:T(2,128)(2,1)}, bf16[1,1408,1536]{2,0,1:T(2,128)(2,1)}, bf16[1,1408,1536]{2,0,1:T(2,128)(2,1)}) fusion(bf16[5,1408,1536]{2,0,1:T(8,128)(2,1)} %all-gather.4.cloned.1.call-done), kind=kLoop, calls=%fused_computation.102 | loop fusion | bytes 43253760 | tf_op jit(solution)/shard_map/slice | solution.py:42
  549.4 0.0 copy-done.4
  549.4 0.0 slice-start
  549.4 0.0 slice-start.1
  549.4 5.0 fusion.7
  554.4 0.0 slice-start.2
  554.5 4.9 fusion.9
  559.4 0.0 slice-done
  559.4 0.0 slice-done.1
  559.4 0.0 slice-done.2
  559.4 1.4 fusion.10
  560.8 0.0 copy-start.1
  560.8 1.4 fusion.11
  562.2 0.0 copy-done.1
  562.3 2.3 fusion.13
  564.6 2.9 reshape.69
  567.5 3.0 reduce_max.9
  570.5 0.2 multiply_reduce_fusion
  570.7 0.0 copy-done.5
  570.7 2.3 convolution_convert_fusion
  573.0 0.0 all-gather.6.cloned.1.call-update
  573.0 0.0 copy-start.2
  573.0 0.1 bitcast_reduce_fusion
  573.2 1.4 convolution_convert_fusion.1
  574.6 16.5 %all_to_all.20 = bf16[32,1,8,128]{3,2,1,0:T(8,128)(2,1)S(1)} all-to-all(bf16[32,1,8,128]{3,2,1,0:T(8,128)(2,1)S(1)} %stack.3), channel_id=1, replica_groups=mesh['dp'=8,'seq'=16,'mp'=2] {'seq','mp'}, dimensions={0} | all-to-all | bytes 131072 | tf_op jit(solution)/shard_map/all_to_all | solution.py:14
  591.1 0.0 copy-start.3
  591.1 0.0 copy-done.2
  591.1 0.1 fusion.55
  591.3 0.5 copy-done.3
  591.8 1.1 copy.31
  592.9 6.5 all-to-all-start.1
  599.4 0.0 all-reduce.3.cloned.1.call-start
  599.4 0.7 broadcast_multiply_fusion
  600.1 0.1 broadcast_bitcast_fusion
  600.1 0.0 copy-done
  600.1 1.3 fusion.52
  601.5 1.8 reshape.70
  603.2 10.9 %all-to-all-done.1 = bf16[1,8,256,128]{3,1,0,2:T(8,128)(2,1)} async-done(((bf16[1,8,256,128]{3,1,0,2:T(8,128)(2,1)}), bf16[1,8,256,128]{3,1,0,2:T(8,128)(2,1)}, u32[]{:S(2)}, u32[]{:S(2)}) %all-to-all-start.1) | async-done | bytes 524320 | tf_op jit(solution)/shard_map/all_to_all | solution.py:109
  614.1 2.2 convolution_bitcast_fusion.1
  616.3 2.3 fusion.51
  618.7 0.0 all-reduce.3.cloned.1.call-update
  618.7 61.4 %all-gather.6.cloned.1.call-done = bf16[4096,320]{0,1:T(8,128)(2,1)} async-done(((bf16[128,320]{0,1:T(8,128)(2,1)}), bf16[4096,320]{0,1:T(8,128)(2,1)}) %all-gather.6.cloned.1.call-update) | async-done | bytes 2621456 | tf_op jit(solution)/shard_map/all_gather | solution.py:102
  680.1 6.6 fusion
  686.7 0.0 copy-done.6
  686.7 5.9 fusion.63
  692.7 2.0 copy.30
  694.7 2.3 reshape.71
  696.9 4.0 fusion.15
  700.9 220.0 %all-reduce.3.cloned.1.call-done = f32[128,128]{1,0:T(8,128)} async-done(((f32[128,128]{1,0:T(8,128)}), f32[128,128]{1,0:T(8,128)}) %all-reduce.3.cloned.1.call-update) | async-done | bytes 65552 | tf_op jit(solution)/shard_map/psum | solution.py:117
  921.0 1.5 copy.69
  (8 shorter events, 0.1 us)
Async XLA Ops:
  7.2 593.0 %copy-start = (bf16[1536,1024]{1,0:T(8,128)(2,1)S(1)}, bf16[1536,1024]{1,0:T(8,128)(2,1)}, u32[]{:S(2)}) copy-start(bf16[1536,1024]{1,0:T(8,128)(2,1)} %param.14) | copy-start | bytes 9437188
  7.2 449.6 %all-gather.4.cloned.1.call-start = ((), (), s32[]{:S(2)}) async-start(), calls=%async_computation.2 | async-start | bytes 35684352 | tf_op jit(solution)/shard_map/all_gather | solution.py:78
  9.9 670.1 %all-gather.6.cloned.1.call-start = ((), (), s32[]{:S(2)}) async-start(), calls=%async_computation.4 | async-start | bytes 2703360 | tf_op jit(solution)/shard_map/all_gather | solution.py:102
  10.7 11.6 %collective-permute-start.1 = (bf16[1,2,1408]{2,1,0:T(2,128)(2,1)S(1)}, bf16[1,2,1408]{2,1,0:T(2,128)(2,1)S(1)}, u32[]{:S(2)}, u32[]{:S(2)}) collective-permute-start(bf16[1,2,1408]{2,1,0:T(2,128)(2,1)S(1)} %get-tuple-element.9), channel_id=1, source_target_pairs={{1,0},{2,1},{3,2},{4,3},{5,4},{6,5},{7,6},{8,7},{9,8},{10,9},{11,1... | collective-permute-start | bytes 16904 | tf_op jit(solution)/shard_map/ppermute | solution.py:25
  12.0 11.0 %collective-permute-start = (bf16[1,2,1408]{2,1,0:T(2,128)(2,1)S(1)}, bf16[1,2,1408]{2,1,0:T(2,128)(2,1)S(1)}, u32[]{:S(2)}, u32[]{:S(2)}) collective-permute-start(bf16[1,2,1408]{2,1,0:T(2,128)(2,1)S(1)} %get-tuple-element.8), channel_id=1, source_target_pairs={{0,1},{1,2},{2,3},{3,4},{4,5},{5,6},{6,7},{7,8},{8,9},{9,10},{10,1... | collective-permute-start | bytes 16904 | tf_op jit(solution)/shard_map/ppermute | solution.py:24
  456.8 92.6 %copy-start.4 = (bf16[260,1408]{1,0:T(8,128)(2,1)S(1)}, bf16[260,1408]{1,0:T(8,128)(2,1)}, u32[]{:S(2)}) copy-start(bf16[260,1408]{1,0:T(8,128)(2,1)} %fusion.20) | copy-start | bytes 2196484
  549.4 9.9 %slice-start = ((s8[8650752]{0:T(1024)(128)(4,1)}), s8[4194304]{0:T(1024)(128)(4,1)S(1)}, s32[]{:S(2)}) async-start(s8[8650752]{0:T(1024)(128)(4,1)} %bitcast.82), calls=%async_computation.5 | async-start | bytes 8388608
  549.4 9.9 %slice-start.1 = ((s8[8650752]{0:T(1024)(128)(4,1)}), s8[4194304]{0:T(1024)(128)(4,1)S(1)}, s32[]{:S(2)}) async-start(s8[8650752]{0:T(1024)(128)(4,1)} %bitcast.82), calls=%async_computation.6 | async-start | bytes 8388608
  554.4 4.9 slice-start.2
  560.8 1.4 copy-start.1
  564.6 6.1 copy-start.5
  573.0 18.1 %copy-start.2 = (bf16[1,8,256,128]{3,2,1,0:T(8,128)(2,1)S(1)}, bf16[1,8,256,128]{3,2,1,0:T(8,128)(2,1)}, u32[]{:S(2)}) copy-start(bf16[1,8,256,128]{3,2,1,0:T(8,128)(2,1)} %param.19) | copy-start | bytes 1572868
  591.1 0.6 copy-start.3
  592.9 21.2 %all-to-all-start.1 = ((bf16[1,8,256,128]{3,1,0,2:T(8,128)(2,1)}), bf16[1,8,256,128]{3,1,0,2:T(8,128)(2,1)}, u32[]{:S(2)}, u32[]{:S(2)}) async-start(bf16[1,8,256,128]{3,1,0,2:T(8,128)(2,1)} %copy.31), calls=%async_computation.1 | async-start | bytes 1048576 | tf_op jit(solution)/shard_map/all_to_all | solution.py:109
  599.4 321.6 %all-reduce.3.cloned.1.call-start = ((), (), s32[]{:S(2)}) async-start(), calls=%async_computation.3 | async-start | bytes 131072 | tf_op jit(solution)/shard_map/psum | solution.py:117
  680.1 6.7 copy-start.6
Sparse Core Ops, SparseCore 0:
  11.4 445.3 all-gather.3
  573.2 106.8 all-gather.5
  686.1 234.7 all-reduce.2
